TPU v7x, 32 devices: a whole 2x2x4 slice. The times are simulated.
32 devices in a mesh: kf: 8 (over z, y), kc: 4 (over x, core).
Axes of the slice: x: 2, y: 2, z: 4, core: 2. Of those that a mesh axis runs over, the one named last changes fastest.
Arguments:
- kernel_coarse: bfloat16 [256, 256], P('kf'), may hold values from -6 to 6
- coefficients: bfloat16 [128, 256], P(('kf', 'kc')), may hold values from -1.5 to 1.5
- nearest: int32 [128], replicated, may hold values from 0 to 15
Outputs:
- kernel_fine: bfloat16 [2048, 2048], P('kf', 'kc')
All inputs are finite; a program needn't handle non-finite values.
Results may differ from a plain program's by a relative error of at most 0.0049.
Values may be sent and summed in bfloat16 or wider, within the bound.
A program may use at most 64 MiB of HBM per device.

v0:
```python
import jax
import jax.numpy as jnp
from jax import lax
from jax.sharding import PartitionSpec as P

P_SIZE = 16


def rotate(kernel_rows, coef_block):
    point_count = coef_block.shape[0]
    pair_count = coef_block.shape[1]
    shaped = kernel_rows.reshape(kernel_rows.shape[0], point_count, pair_count)
    turned = jnp.einsum("ckn,kan->cka", shaped, coef_block, preferred_element_type=jnp.float32)
    return turned.astype(jnp.bfloat16).reshape(kernel_rows.shape[0], point_count * pair_count)


def shards(kernel_coarse, coefficients, nearest):
    pair_count = P_SIZE
    total_rows = kernel_coarse.shape[1]
    fine_total = nearest.shape[0]
    slab_size = fine_total // lax.axis_size("kf")
    kc_count = lax.axis_size("kc")
    part_index = lax.axis_index("kc")
    offsets = jnp.arange(pair_count, dtype=jnp.int32)
    coef_whole = lax.all_gather(coefficients, ("kf", "kc"), axis=0, tiled=True).reshape(
        fine_total, pair_count, pair_count
    )
    share_size = slab_size // kc_count
    grouped = nearest.reshape(lax.axis_size("kf"), kc_count, share_size)
    chosen = lax.dynamic_index_in_dim(grouped, part_index, 1, keepdims=False)
    columns = (chosen.reshape(-1)[:, None] * pair_count + offsets[None, :]).reshape(-1)
    outgoing = jnp.take(kernel_coarse, columns, axis=1)
    received = lax.all_to_all(outgoing, "kf", split_axis=1, concat_axis=0, tiled=True)
    own_coef = coefficients.reshape(share_size, pair_count, pair_count)
    turned = rotate(received, own_coef)
    rotated = lax.all_gather(turned, "kc", axis=1, tiled=True)
    col_total = fine_total // kc_count
    col_coarse = lax.dynamic_slice_in_dim(nearest, part_index * col_total, col_total)
    coef_cols = lax.dynamic_slice_in_dim(coef_whole, part_index * col_total, col_total, 0)
    stacked = rotated.reshape(total_rows // pair_count, pair_count, rotated.shape[1])
    picked = jnp.take(stacked, col_coarse, axis=0)
    result = jnp.einsum("jnr,jbn->rjb", picked, coef_cols, preferred_element_type=jnp.float32)
    return result.reshape(result.shape[0], col_total * pair_count).astype(jnp.bfloat16)


def solution(mesh):
    in_specs = (P("kf", None), P(("kf", "kc"), None), P())
    out_specs = P("kf", "kc")
    return jax.shard_map(shards, mesh=mesh, in_specs=in_specs, out_specs=out_specs, check_vma=False)
```

profile of v0, /device:TPU:0, one launch (start us, length us, event | category | flops | bytes accessed | tf_op | source)
XLA Modules:
  0.0 63.8 jit_solution(2334305354638408349)
XLA Ops:
  0.0 0.7 %copy-done.2 = s32[128]{0:T(128)S(1)} copy-done((s32[128]{0:T(128)S(1)}, s32[128]{0:T(128)}, u32[]{:S(2)}) %copy-start.2) | copy-done | bytes 536
  0.7 0.1 reshape.90
  0.8 0.5 broadcast.58
  1.3 0.7 %fusion.6 = (s32[8,4]{1,0:T(8,128)S(1)}, s32[8,1,4]{2,1,0:T(1,128)S(1)}) fusion(s32[]{:T(128)} %broadcast.58, s32[8,4,4]{2,1,0:T(4,128)S(1)} %reshape.90, s32[]{:T(128)S(6)} %select_n.41), kind=kLoop, calls=%fused_computation.20 | loop fusion | flops 32 | bytes 392 | tf_op jit(solution)/shard_map/mul | solution.py:31
  2.1 0.1 add.83
  2.5 0.6 copy-done
  3.1 0.1 copy.17
  3.2 1.3 %gather_fusion = bf16[512,32]{1,0:T(8,128)(2,1)S(1)} fusion(bf16[32,256]{0,1:T(8,128)(2,1)S(1)} %copy.17, s32[1024]{0:T(1024)S(1)} %pad_clamp_fusion.1), kind=kCustom, calls=%fused_computation | custom fusion | bytes 67584 | tf_op jit(solution)/shard_map/jit(_take)/gather | solution.py:32
  4.6 0.1 copy.18
  4.7 0.7 %reshape.124 = bf16[8,2,1024]{2,1,0:T(2,128)(2,1)} reshape(bf16[8,32,64]{2,1,0:T(8,128)(2,1)S(1)} %fusion.7) | data formatting | bytes 65536
  5.4 7.3 %all-to-all-start = ((bf16[8,2,1024]{2,1,0:T(2,128)(2,1)}), bf16[8,2,1024]{2,1,0:T(2,128)(2,1)S(1)}, u32[]{:S(2)}, u32[]{:S(2)}) async-start(bf16[8,2,1024]{2,1,0:T(2,128)(2,1)} %reshape.124), calls=%async_computation | async-start | bytes 65536 | tf_op jit(solution)/shard_map/all_to_all | solution.py:33
  12.8 0.6 copy-done.1
  13.4 0.1 reshape.92
  13.5 42.1 %all-gather = bf16[32,4,256]{2,1,0:T(4,128)(2,1)S(1)} all-gather(bf16[1,4,256]{2,1,0:T(4,128)(2,1)S(1)} %bitcast.28), channel_id=1, replica_groups=mesh['kf'=8,'kc'=4] {'kf','kc'}, dimensions={0}, use_global_device_ids=true | all-gather | bytes 67584 | tf_op jit(solution)/shard_map/all_gather | solution.py:25
  55.6 0.4 reshape.89
  56.0 0.1 reshape.125
  56.1 0.1 copy.19
  56.3 0.1 reshape.91
  56.4 0.1 convolution_convert_fusion.1
  56.5 5.4 %all_gather.7 = bf16[256,256]{0,1:T(8,128)(2,1)S(1)} all-gather(bf16[256,64]{0,1:T(8,128)(2,1)S(1)} %bitcast.26), channel_id=1, replica_groups=mesh['kf'=8,'kc'=4] {'kc'}, dimensions={1}, use_global_device_ids=true | all-gather | bytes 163840 | tf_op jit(solution)/shard_map/all_gather | solution.py:36
  61.9 0.1 copy.20
  62.1 0.6 gather_fusion.1
  62.6 0.3 convolution_convert_fusion
  62.9 0.8 %copy.21 = bf16[256,512]{1,0:T(8,128)(2,1)} copy(bf16[256,512]{0,1:T(8,128)(2,1)S(1)} %bitcast.24) | data formatting | bytes 524288 | tf_op jit(solution)/shard_map/convert_element_type | solution.py:43
  (17 shorter events, 0.5 us)
Async XLA Ops:
  0.0 0.7 %copy-start.2 = (s32[128]{0:T(128)S(1)}, s32[128]{0:T(128)}, u32[]{:S(2)}) copy-start(s32[128]{0:T(128)} %param.5) | copy-start | bytes 1540
  2.4 0.7 %copy-start = (bf16[32,256]{1,0:T(8,128)(2,1)S(1)}, bf16[32,256]{1,0:T(8,128)(2,1)}, u32[]{:S(2)}) copy-start(bf16[32,256]{1,0:T(8,128)(2,1)} %param.3) | copy-start | bytes 49156
  5.4 50.6 %all-to-all-start = ((bf16[8,2,1024]{2,1,0:T(2,128)(2,1)}), bf16[8,2,1024]{2,1,0:T(2,128)(2,1)S(1)}, u32[]{:S(2)}, u32[]{:S(2)}) async-start(bf16[8,2,1024]{2,1,0:T(2,128)(2,1)} %reshape.124), calls=%async_computation | async-start | bytes 65536 | tf_op jit(solution)/shard_map/all_to_all | solution.py:33
  12.8 0.7 %copy-start.1 = (bf16[4,256]{1,0:T(4,128)(2,1)S(1)}, bf16[4,256]{1,0:T(4,128)(2,1)}, u32[]{:S(2)}) copy-start(bf16[4,256]{1,0:T(4,128)(2,1)} %param.4) | copy-start | bytes 6148
where the time goes:
time: 64.1 us; the launch traced here: 63.8 us
  blocking collectives  47.5 us (74%)
  local copies, waits for them, and re-layouts  7.54 us (12%)
  starting transfers between devices  7.31 us (11%)
  other arithmetic  0.86 us (1%)
    all_gather x1, blocking collectives, shards(): lax.all_gather(coefficients, ('kf', 'kc'), axis=0, tiled=True)  42.1 us
    all_to_all x1, starting transfers between devices, shards(): lax.all_to_all(outgoing, 'kf', split_axis=1, concat_axis=0, tiled=True)  7.31 us
    all_gather x1, blocking collectives, shards(): rotated = lax.all_gather(turned, 'kc', axis=1, tiled=True)  5.41 us
    unnamed x9, local copies, waits for them, and re-layouts  2.83 us
    gather x2, local copies, waits for them, and re-layouts, shards(): outgoing = jnp.take(kernel_coarse, columns, axis=1)  1.45 us
  transfers between devices with their start and end apart: 1, of which 0 were waited for; matrix products, arithmetic and copies ran while one was open for 1% of the time, Pallas kernels for 0%

commit v1 on v0

v1 whole, which is shorter than its diff:
```python
import functools
import math

import jax
import jax.numpy as jnp
from jax import lax
from jax.experimental import pallas as pl
from jax.experimental.pallas import tpu as pltpu
from jax.sharding import PartitionSpec as P

UNROLL_LIMIT = 16
CHUNK_SLOTS = 8


def each(low, high, step):
    if high - low <= UNROLL_LIMIT:
        for index in range(low, high):
            step(index)
    else:
        lax.fori_loop(low, high, lambda index, carry: (step(index), carry)[1], 0)


def remote(source, target, send_sem, recv_sem, kf, kc):
    return pltpu.make_async_remote_copy(
        src_ref=source,
        dst_ref=target,
        send_sem=send_sem,
        recv_sem=recv_sem,
        device_id={"kf": kf, "kc": kc},
        device_id_type=pl.DeviceIdType.MESH,
    )


def signal(barrier, kf, kc):
    pl.semaphore_signal(
        barrier, inc=1, device_id={"kf": kf, "kc": kc}, device_id_type=pl.DeviceIdType.MESH
    )


def expand(blocks, near, first_point, spread, target):
    slot_count, points, width = blocks.shape
    pairs = math.isqrt(width)
    column_total = target.shape[1]
    chunk = min(slot_count, CHUNK_SLOTS)
    own_block = (
        lax.broadcasted_iota(jnp.int32, (pairs, width), 1) // pairs
        == lax.broadcasted_iota(jnp.int32, (pairs, width), 0)
    )
    coarse_of = lax.broadcasted_iota(jnp.int32, (pairs, column_total), 1) // pairs
    fold = (
        lax.broadcasted_iota(jnp.int32, (width, column_total), 0) % pairs
        == lax.broadcasted_iota(jnp.int32, (width, column_total), 1) % pairs
    ).astype(jnp.bfloat16)
    chunk_points = chunk * points

    def step(part):
        for slot in range(chunk):
            block = blocks[part * chunk + slot].astype(jnp.float32)
            for point in range(points):
                row = jnp.broadcast_to(block[point : point + 1, :], (pairs, width))
                place = (slot * points + point) * pairs
                spread[place : place + pairs, :] = jnp.where(own_block, row, 0.0).astype(jnp.bfloat16)
        tiled = jnp.dot(
            spread[: chunk_points * pairs, :], fold, preferred_element_type=jnp.float32
        )
        for point in range(chunk_points):
            place = point * pairs
            wanted = near[first_point + part * chunk_points + point]
            kept = jnp.where(coarse_of == wanted, tiled[place : place + pairs, :], 0.0)
            offset = part * (chunk_points * pairs) + place
            if not isinstance(part, int):
                offset = pl.multiple_of(offset, pairs)
            target[pl.ds(offset, pairs), :] = kept.astype(jnp.bfloat16)

    parts = slot_count // chunk
    if parts == 1:
        step(0)
    else:
        lax.fori_loop(0, parts, lambda part, carry: (step(part), carry)[1], 0)


def kernel(
    kf_count, kc_count, kernel_hbm, coef_hbm, near_hbm, turned_ref, columns_ref,
    kernel_all, coef_slab, coef_cols, near, spread, factor,
    local_sem, kernel_send, kernel_recv, slab_send, slab_recv, cols_send, cols_recv,
):
    kf, kc = lax.axis_index("kf"), lax.axis_index("kc")
    group = kf_count // kc_count
    points = coef_hbm.shape[0]
    slab_points = points * kc_count
    column_points = coef_cols.shape[0] * points
    part = kf // group
    in_part = part == kc
    slot = (kf % group) * kc_count + kc

    near_copy = pltpu.make_async_copy(near_hbm, near, local_sem.at[0])
    kernel_copy = pltpu.make_async_copy(kernel_hbm, kernel_all.at[kf], local_sem.at[1])
    coef_copy = pltpu.make_async_copy(coef_hbm, coef_slab.at[kc], local_sem.at[2])
    cols_copy = pltpu.make_async_copy(coef_hbm, coef_cols.at[slot], cols_recv.at[slot])
    coef_copy.start()
    kernel_copy.start()
    near_copy.start()

    @pl.when(in_part)
    def _():
        cols_copy.start()

    barrier = pltpu.get_barrier_semaphore()
    each(1, kf_count, lambda t: signal(barrier, lax.rem(kf + t, kf_count), kc))
    each(1, kc_count, lambda t: signal(barrier, kf, lax.rem(kc + t, kc_count)))

    def greet(index):
        source_kf = kc * group + index // kc_count
        source_kc = index % kc_count

        @pl.when(jnp.logical_or(source_kf != kf, source_kc != kc))
        def _():
            signal(barrier, source_kf, source_kc)

    each(0, group * kc_count, greet)
    coef_copy.wait()
    kernel_copy.wait()
    pl.semaphore_wait(barrier, 2 * kf_count + kc_count - 2 - in_part.astype(jnp.int32))

    def slab_to(t):
        return remote(
            coef_slab.at[kc], coef_slab.at[kc], slab_send.at[t], slab_recv.at[kc],
            kf, lax.rem(kc + t, kc_count),
        )

    def cols_to(t):
        return remote(
            coef_slab.at[kc], coef_cols.at[slot], cols_send.at[t], cols_recv.at[slot],
            lax.rem(kf + t, kf_count), part,
        )

    def kernel_to(t):
        return remote(
            kernel_all.at[kf], kernel_all.at[kf], kernel_send.at[t], kernel_recv.at[kf],
            lax.rem(kf + t, kf_count), kc,
        )

    each(1, kf_count, lambda t: cols_to(t).start())

    @pl.when(jnp.logical_not(in_part))
    def _():
        cols_to(0).start()

    each(1, kc_count, lambda t: slab_to(t).start())
    each(1, kf_count, lambda t: kernel_to(t).start())
    near_copy.wait()

    def slab_from(t):
        source = lax.rem(kc + t, kc_count)
        remote(
            coef_slab.at[source], coef_slab.at[source], slab_send.at[t], slab_recv.at[source],
            kf, source,
        ).wait_recv()

    each(1, kc_count, slab_from)
    expand(coef_slab, near, kf * slab_points, spread, factor)

    def cols_from(index):
        pltpu.make_async_copy(coef_hbm, coef_cols.at[index], cols_recv.at[index]).wait()

    each(0, group * kc_count, cols_from)
    expand(coef_cols, near, kc * column_points, spread, columns_ref)

    def kernel_from(t):
        source = lax.rem(kf + t, kf_count)
        remote(
            kernel_all.at[source], kernel_all.at[source], kernel_send.at[t], kernel_recv.at[source],
            source, kc,
        ).wait_recv()

    each(1, kf_count, kernel_from)
    own_rows, width = kernel_hbm.shape
    chunk = min(kf_count, CHUNK_SLOTS)

    def rotate(index):
        rows = kernel_all[pl.ds(index * chunk, chunk)].reshape(chunk * own_rows, width)
        turned = lax.dot_general(
            factor[...], rows, (((1,), (1,)), ((), ())), preferred_element_type=jnp.float32
        )
        offset = index * (chunk * own_rows)
        if not isinstance(index, int):
            offset = pl.multiple_of(offset, chunk * own_rows)
        turned_ref[:, pl.ds(offset, chunk * own_rows)] = turned.astype(jnp.bfloat16)

    parts = kf_count // chunk
    if parts == 1:
        rotate(0)
    else:
        lax.fori_loop(0, parts, lambda index, carry: (rotate(index), carry)[1], 0)

    each(1, kf_count, lambda t: cols_to(t).wait_send())

    @pl.when(jnp.logical_not(in_part))
    def _():
        cols_to(0).wait_send()

    each(1, kc_count, lambda t: slab_to(t).wait_send())
    each(1, kf_count, lambda t: kernel_to(t).wait_send())


def shards(kf_count, kc_count, kernel_coarse, coefficients, nearest):
    own_rows, width = kernel_coarse.shape
    points, entries = coefficients.shape
    pairs = math.isqrt(entries)
    slots = kf_count // kc_count * kc_count
    slab_rows = kc_count * points * pairs
    column_rows = slots * points * pairs
    spread_rows = max(min(kc_count, CHUNK_SLOTS), min(slots, CHUNK_SLOTS)) * points * pairs
    dma = pltpu.SemaphoreType.DMA
    turned, columns = pl.pallas_call(
        functools.partial(kernel, kf_count, kc_count),
        out_shape=(
            jax.ShapeDtypeStruct((slab_rows, kf_count * own_rows), jnp.bfloat16),
            jax.ShapeDtypeStruct((column_rows, width), jnp.bfloat16),
        ),
        in_specs=[pl.BlockSpec(memory_space=pl.ANY)] * 3,
        out_specs=(pl.BlockSpec(memory_space=pltpu.VMEM), pl.BlockSpec(memory_space=pltpu.VMEM)),
        scratch_shapes=[
            pltpu.VMEM((kf_count, own_rows, width), jnp.bfloat16),
            pltpu.VMEM((kc_count, points, entries), jnp.bfloat16),
            pltpu.VMEM((slots, points, entries), jnp.bfloat16),
            pltpu.SMEM(nearest.shape, jnp.int32),
            pltpu.VMEM((spread_rows, entries), jnp.bfloat16),
            pltpu.VMEM((slab_rows, width), jnp.bfloat16),
            dma((3,)),
            dma((kf_count,)),
            dma((kf_count,)),
            dma((kc_count,)),
            dma((kc_count,)),
            dma((kf_count,)),
            dma((slots,)),
        ],
        compiler_params=pltpu.CompilerParams(collective_id=0, has_side_effects=True),
    )(kernel_coarse, coefficients, nearest)
    result = lax.dot_general(
        turned, columns, (((1,), (1,)), ((), ())), preferred_element_type=jnp.float32
    )
    return result.astype(jnp.bfloat16)


def solution(mesh):
    body = functools.partial(shards, mesh.shape["kf"], mesh.shape["kc"])
    in_specs = (P("kf", None), P(("kf", "kc"), None), P())
    return jax.shard_map(body, mesh=mesh, in_specs=in_specs, out_specs=P("kf", "kc"), check_vma=False)
```

time: 64.1 us -> 14.3 us (0.22)
  blocking collectives: 47.5 us -> 0 us
  Pallas kernels: 0 us -> 12.1 us
  local copies, waits for them, and re-layouts: 7.54 us -> 0 us
  starting transfers between devices: 7.31 us -> 0 us
  matrix products: 0.4 us -> 1.99 us
  other arithmetic: 0.86 us -> 0 us
    all_gather x2 -> x0, blocking collectives: 47.5 us -> none  [the longest x1 42.1 us: shards(): lax.all_gather(coefficients, ('kf', 'kc'), axis=0, tiled=True)]
    pallas_call x0 -> x1, Pallas kernels: none -> 12.1 us  [shards(): pl.pallas_call(functools.partial(kernel, kf_count, kc_count), out_shape=(...]
    all_to_all x1 -> x0, starting transfers between devices: 7.31 us -> none  [shards(): lax.all_to_all(outgoing, 'kf', split_axis=1, concat_axis=0, tiled=True)]
    unnamed x9 -> x0, local copies, waits for them, and re-layouts: 2.83 us -> none
    gather x3 -> x0, local copies, waits for them, and re-layouts: 2.02 us -> none  [the longest x2 1.45 us: shards(): outgoing = jnp.take(kernel_coarse, columns, axis=1)]
    dot_general x2 -> x1, matrix products: 0.4 us -> 1.99 us  [shards(): lax.dot_general(turned, columns, (((1,), (1,)), ((), ())), preferred_elem...]
    convert_element_type x1 -> x0, local copies, waits for them, and re-layouts: 0.85 us -> none  [shards(): result.reshape(result.shape[0], col_total * pair_count).astype(jnp.bfloat16)]
    reshape x4 -> x0, local copies, waits for them, and re-layouts: 0.69 us -> none  [the longest x1 0.37 us: shards(): lax.all_gather(coefficients, ('kf', 'kc'), axis=0, tiled=True)]
  transfers between devices with their start and end apart: 1 -> 0, of which waited for: 0 -> 0; matrix products, arithmetic and copies ran while one was open for 1% -> 0% of each run, Pallas kernels for 0% -> 0%
where the time goes in v1:
time: 14.3 us; the launch traced here: 14.1 us
  Pallas kernels  12.1 us (85%)
  matrix products  1.99 us (14%)
    pallas_call x1, Pallas kernels, shards(): pl.pallas_call(functools.partial(kernel, kf_count, kc_count), out_shape=(...  12.1 us
    dot_general x1, matrix products, shards(): lax.dot_general(turned, columns, (((1,), (1,)), ((), ())), preferred_elem...  1.99 us

profile of v1, /device:TPU:0, one launch (start us, length us, event | category | flops | bytes accessed | tf_op | source)
XLA Modules:
  0.0 14.1 jit_solution(16742262090167128069)
XLA Ops:
  0.0 12.1 %shard_map.37 = (bf16[256,256]{1,0:T(8,128)(2,1)}, bf16[512,256]{1,0:T(8,128)(2,1)}) custom-call(bf16[32,256]{1,0:T(8,128)(2,1)} %kernel_hbm.1, bf16[4,256]{1,0:T(4,128)(2,1)} %coef_hbm.1, s32[128]{0:T(128)} %near_hbm.1), custom_call_target="tpu_custom_call" | custom-call | tf_op jit(solution)/shard_map/pallas_call | solution.py:215
  12.1 2.0 %convolution_convert_fusion = bf16[256,512]{1,0:T(8,128)(2,1)} fusion(bf16[256,256]{1,0:T(8,128)(2,1)} %get-tuple-element.7, bf16[512,256]{1,0:T(8,128)(2,1)} %get-tuple-element.8), kind=kOutput, calls=%fused_computation | convolution fusion | flops 67239936 | bytes 655360 | tf_op jit(solution)/shard_map/dot_general | solution.py:240

commit v2 on v1

--- a/solution.py
+++ b/solution.py
@@ -10,6 +10,7 @@
 
 UNROLL_LIMIT = 16
 CHUNK_SLOTS = 8
+VMEM_ELEMENTS = 1 << 20
 
 
 def each(low, high, step):
@@ -83,6 +84,7 @@
     kf_count, kc_count, kernel_hbm, coef_hbm, near_hbm, turned_ref, columns_ref,
     kernel_all, coef_slab, coef_cols, near, spread, factor,
     local_sem, kernel_send, kernel_recv, slab_send, slab_recv, cols_send, cols_recv,
+    kernel_ready, slab_ready, cols_ready,
 ):
     kf, kc = lax.axis_index("kf"), lax.axis_index("kc")
     group = kf_count // kc_count
@@ -106,58 +108,81 @@
         cols_copy.start()
 
     barrier = pltpu.get_barrier_semaphore()
-    each(1, kf_count, lambda t: signal(barrier, lax.rem(kf + t, kf_count), kc))
-    each(1, kc_count, lambda t: signal(barrier, kf, lax.rem(kc + t, kc_count)))
-
-    def greet(index):
-        source_kf = kc * group + index // kc_count
-        source_kc = index % kc_count
-
-        @pl.when(jnp.logical_or(source_kf != kf, source_kc != kc))
-        def _():
-            signal(barrier, source_kf, source_kc)
-
-    each(0, group * kc_count, greet)
+    rank = kf * kc_count + kc
+    source_count = group * kc_count
+    first_source = kc * source_count
+
+    def when(condition, step):
+        pl.when(condition)(step)
+
+    def greet_kf(p):
+        when(p > kf, lambda: signal(barrier, p, kc))
+        when(p * kc_count + part > rank, lambda: signal(barrier, p, part))
+
+    def source_of(index):
+        return kc * group + index // kc_count, index % kc_count
+
+    each(0, kf_count, greet_kf)
+    each(0, kc_count, lambda q: when(q > kc, lambda: signal(barrier, kf, q)))
+    each(0, source_count, lambda n: when(first_source + n > rank, lambda: signal(barrier, *source_of(n))))
+    lower_sources = jnp.clip(rank - first_source, 0, source_count)
     coef_copy.wait()
     kernel_copy.wait()
-    pl.semaphore_wait(barrier, 2 * kf_count + kc_count - 2 - in_part.astype(jnp.int32))
-
-    def slab_to(t):
+    greetings = 2 * kf + kc + (part < kc).astype(jnp.int32) + lower_sources
+    when(greetings > 0, lambda: pl.semaphore_wait(barrier, greetings))
+
+    each(0, kf_count, lambda p: when(p < kf, lambda: signal(kernel_ready.at[kf], p, kc)))
+    each(0, source_count, lambda n: when(first_source + n < rank, lambda: signal(cols_ready.at[kf], *source_of(n))))
+    each(0, kc_count, lambda q: when(q < kc, lambda: signal(slab_ready.at[kc], kf, q)))
+
+    def slab_to(q):
         return remote(
-            coef_slab.at[kc], coef_slab.at[kc], slab_send.at[t], slab_recv.at[kc],
-            kf, lax.rem(kc + t, kc_count),
-        )
-
-    def cols_to(t):
+            coef_slab.at[kc], coef_slab.at[kc], slab_send.at[q], slab_recv.at[kc], kf, q
+        )
+
+    def cols_to(p):
         return remote(
-            coef_slab.at[kc], coef_cols.at[slot], cols_send.at[t], cols_recv.at[slot],
-            lax.rem(kf + t, kf_count), part,
-        )
-
-    def kernel_to(t):
+            coef_slab.at[kc], coef_cols.at[slot], cols_send.at[p], cols_recv.at[slot], p, part
+        )
+
+    def kernel_to(p):
         return remote(
-            kernel_all.at[kf], kernel_all.at[kf], kernel_send.at[t], kernel_recv.at[kf],
-            lax.rem(kf + t, kf_count), kc,
-        )
-
-    each(1, kf_count, lambda t: cols_to(t).start())
-
-    @pl.when(jnp.logical_not(in_part))
-    def _():
-        cols_to(0).start()
-
-    each(1, kc_count, lambda t: slab_to(t).start())
-    each(1, kf_count, lambda t: kernel_to(t).start())
+            kernel_all.at[kf], kernel_all.at[kf], kernel_send.at[p], kernel_recv.at[kf], p, kc
+        )
+
+    def send_lower(p):
+        when(p * kc_count + part < rank, lambda: cols_to(p).start())
+        when(p < kf, lambda: kernel_to(p).start())
+
+    def send_higher(p):
+        @pl.when(p * kc_count + part > rank)
+        def _():
+            pl.semaphore_wait(cols_ready.at[p], 1)
+            cols_to(p).start()
+
+        @pl.when(p > kf)
+        def _():
+            pl.semaphore_wait(kernel_ready.at[p], 1)
+            kernel_to(p).start()
+
+    def slab_higher(q):
+        @pl.when(q > kc)
+        def _():
+            pl.semaphore_wait(slab_ready.at[q], 1)
+            slab_to(q).start()
+
+    each(0, kf_count, send_lower)
+    each(0, kc_count, lambda q: when(q < kc, lambda: slab_to(q).start()))
+    each(0, kc_count, slab_higher)
+    each(0, kf_count, send_higher)
     near_copy.wait()
 
-    def slab_from(t):
-        source = lax.rem(kc + t, kc_count)
-        remote(
-            coef_slab.at[source], coef_slab.at[source], slab_send.at[t], slab_recv.at[source],
-            kf, source,
-        ).wait_recv()
-
-    each(1, kc_count, slab_from)
+    def slab_from(q):
+        when(q != kc, lambda: remote(
+            coef_slab.at[q], coef_slab.at[q], slab_send.at[q], slab_recv.at[q], kf, q
+        ).wait_recv())
+
+    each(0, kc_count, slab_from)
     expand(coef_slab, near, kf * slab_points, spread, factor)
 
     def cols_from(index):
@@ -166,14 +191,12 @@
     each(0, group * kc_count, cols_from)
     expand(coef_cols, near, kc * column_points, spread, columns_ref)
 
-    def kernel_from(t):
-        source = lax.rem(kf + t, kf_count)
-        remote(
-            kernel_all.at[source], kernel_all.at[source], kernel_send.at[t], kernel_recv.at[source],
-            source, kc,
-        ).wait_recv()
-
-    each(1, kf_count, kernel_from)
+    def kernel_from(p):
+        when(p != kf, lambda: remote(
+            kernel_all.at[p], kernel_all.at[p], kernel_send.at[p], kernel_recv.at[p], p, kc
+        ).wait_recv())
+
+    each(0, kf_count, kernel_from)
     own_rows, width = kernel_hbm.shape
     chunk = min(kf_count, CHUNK_SLOTS)
 
@@ -193,14 +216,12 @@
     else:
         lax.fori_loop(0, parts, lambda index, carry: (rotate(index), carry)[1], 0)
 
-    each(1, kf_count, lambda t: cols_to(t).wait_send())
-
-    @pl.when(jnp.logical_not(in_part))
-    def _():
-        cols_to(0).wait_send()
-
-    each(1, kc_count, lambda t: slab_to(t).wait_send())
-    each(1, kf_count, lambda t: kernel_to(t).wait_send())
+    def sent(p):
+        when(p * kc_count + part != rank, lambda: cols_to(p).wait_send())
+        when(p != kf, lambda: kernel_to(p).wait_send())
+
+    each(0, kf_count, sent)
+    each(0, kc_count, lambda q: when(q != kc, lambda: slab_to(q).wait_send()))
 
 
 def shards(kf_count, kc_count, kernel_coarse, coefficients, nearest):
@@ -211,12 +232,14 @@
     slab_rows = kc_count * points * pairs
     column_rows = slots * points * pairs
     spread_rows = max(min(kc_count, CHUNK_SLOTS), min(slots, CHUNK_SLOTS)) * points * pairs
-    dma = pltpu.SemaphoreType.DMA
+    dma, regular = pltpu.SemaphoreType.DMA, pltpu.SemaphoreType.REGULAR
+    fits = (slab_rows + column_rows) * width <= VMEM_ELEMENTS
+    place = pltpu.VMEM if fits else jax.ShapeDtypeStruct
     turned, columns = pl.pallas_call(
         functools.partial(kernel, kf_count, kc_count),
         out_shape=(
-            jax.ShapeDtypeStruct((slab_rows, kf_count * own_rows), jnp.bfloat16),
-            jax.ShapeDtypeStruct((column_rows, width), jnp.bfloat16),
+            place((slab_rows, kf_count * own_rows), jnp.bfloat16),
+            place((column_rows, width), jnp.bfloat16),
         ),
         in_specs=[pl.BlockSpec(memory_space=pl.ANY)] * 3,
         out_specs=(pl.BlockSpec(memory_space=pltpu.VMEM), pl.BlockSpec(memory_space=pltpu.VMEM)),
@@ -234,6 +257,9 @@
             dma((kc_count,)),
             dma((kf_count,)),
             dma((slots,)),
+            regular((kf_count,)),
+            regular((kc_count,)),
+            regular((kf_count,)),
         ],
         compiler_params=pltpu.CompilerParams(collective_id=0, has_side_effects=True),
     )(kernel_coarse, coefficients, nearest)

time: 14.3 us -> 11.6 us (0.81)
  Pallas kernels: 12.1 us -> 10.5 us
  matrix products: 1.99 us -> 0.97 us
    pallas_call x1, Pallas kernels: 12.1 us -> 10.5 us  [shards(): pl.pallas_call(functools.partial(kernel, kf_count, kc_count), out_shape=(...]
    dot_general x1, matrix products: 1.99 us -> 0.97 us  [shards(): lax.dot_general(turned, columns, (((1,), (1,)), ((), ())), preferred_elem...]
where the time goes in v2:
time: 11.6 us; the launch traced here: 11.5 us
  Pallas kernels  10.5 us (91%)
  matrix products  0.97 us (8%)
    pallas_call x1, Pallas kernels, shards(): pl.pallas_call(functools.partial(kernel, kf_count, kc_count), out_shape=(...  10.5 us
    dot_general x1, matrix products, shards(): lax.dot_general(turned, columns, (((1,), (1,)), ((), ())), preferred_elem...  0.97 us

profile of v2, /device:TPU:0, one launch (start us, length us, event | category | flops | bytes accessed | tf_op | source)
XLA Modules:
  0.0 11.5 jit_solution(8387890159237579533)
XLA Ops:
  0.0 10.5 %shard_map.37 = (bf16[256,256]{1,0:T(8,128)(2,1)S(1)}, bf16[512,256]{1,0:T(8,128)(2,1)S(1)}) custom-call(bf16[32,256]{1,0:T(8,128)(2,1)} %kernel_hbm.1, bf16[4,256]{1,0:T(4,128)(2,1)} %coef_hbm.1, s32[128]{0:T(128)} %near_hbm.1), custom_call_target="tpu_custom_call" | custom-call | tf_op jit(solution)/shard_map/pallas_call | solution.py:238
  10.5 1.0 %convolution_convert_fusion = bf16[256,512]{1,0:T(8,128)(2,1)} fusion(bf16[256,256]{1,0:T(8,128)(2,1)S(1)} %get-tuple-element.7, bf16[512,256]{1,0:T(8,128)(2,1)S(1)} %get-tuple-element.8), kind=kOutput, calls=%fused_computation | convolution fusion | flops 67239936 | bytes 655360 | tf_op jit(solution)/shard_map/dot_general | solution.py:266

commit v3 on v2

--- a/solution.py
+++ b/solution.py
@@ -38,7 +38,7 @@
     )
 
 
-def expand(blocks, near, first_point, spread, target):
+def expand(blocks, near, first_point, spread, fold, target):
     slot_count, points, width = blocks.shape
     pairs = math.isqrt(width)
     column_total = target.shape[1]
@@ -48,10 +48,6 @@
         == lax.broadcasted_iota(jnp.int32, (pairs, width), 0)
     )
     coarse_of = lax.broadcasted_iota(jnp.int32, (pairs, column_total), 1) // pairs
-    fold = (
-        lax.broadcasted_iota(jnp.int32, (width, column_total), 0) % pairs
-        == lax.broadcasted_iota(jnp.int32, (width, column_total), 1) % pairs
-    ).astype(jnp.bfloat16)
     chunk_points = chunk * points
 
     def step(part):
@@ -62,7 +58,7 @@
                 place = (slot * points + point) * pairs
                 spread[place : place + pairs, :] = jnp.where(own_block, row, 0.0).astype(jnp.bfloat16)
         tiled = jnp.dot(
-            spread[: chunk_points * pairs, :], fold, preferred_element_type=jnp.float32
+            spread[: chunk_points * pairs, :], fold[...], preferred_element_type=jnp.float32
         )
         for point in range(chunk_points):
             place = point * pairs
@@ -82,7 +78,7 @@
 
 def kernel(
     kf_count, kc_count, kernel_hbm, coef_hbm, near_hbm, turned_ref, columns_ref,
-    kernel_all, coef_slab, coef_cols, near, spread, factor,
+    kernel_all, coef_slab, coef_cols, near, spread, fold, factor,
     local_sem, kernel_send, kernel_recv, slab_send, slab_recv, cols_send, cols_recv,
     kernel_ready, slab_ready, cols_ready,
 ):
@@ -126,6 +122,11 @@
     each(0, kc_count, lambda q: when(q > kc, lambda: signal(barrier, kf, q)))
     each(0, source_count, lambda n: when(first_source + n > rank, lambda: signal(barrier, *source_of(n))))
     lower_sources = jnp.clip(rank - first_source, 0, source_count)
+    pairs = math.isqrt(coef_hbm.shape[1])
+    fold[...] = (
+        lax.broadcasted_iota(jnp.int32, fold.shape, 0) % pairs
+        == lax.broadcasted_iota(jnp.int32, fold.shape, 1) % pairs
+    ).astype(jnp.bfloat16)
     coef_copy.wait()
     kernel_copy.wait()
     greetings = 2 * kf + kc + (part < kc).astype(jnp.int32) + lower_sources
@@ -183,13 +184,13 @@
         ).wait_recv())
 
     each(0, kc_count, slab_from)
-    expand(coef_slab, near, kf * slab_points, spread, factor)
+    expand(coef_slab, near, kf * slab_points, spread, fold, factor)
 
     def cols_from(index):
         pltpu.make_async_copy(coef_hbm, coef_cols.at[index], cols_recv.at[index]).wait()
 
     each(0, group * kc_count, cols_from)
-    expand(coef_cols, near, kc * column_points, spread, columns_ref)
+    expand(coef_cols, near, kc * column_points, spread, fold, columns_ref)
 
     def kernel_from(p):
         when(p != kf, lambda: remote(
@@ -249,6 +250,7 @@
             pltpu.VMEM((slots, points, entries), jnp.bfloat16),
             pltpu.SMEM(nearest.shape, jnp.int32),
             pltpu.VMEM((spread_rows, entries), jnp.bfloat16),
+            pltpu.VMEM((entries, width), jnp.bfloat16),
             pltpu.VMEM((slab_rows, width), jnp.bfloat16),
             dma((3,)),
             dma((kf_count,)),

time: 11.6 us -> 11.6 us (level)
  no operation moved by 1% of the time
where the time goes in v3:
time: 11.6 us; the launch traced here: 11.5 us
  Pallas kernels  10.5 us (91%)
  matrix products  0.97 us (8%)
    pallas_call x1, Pallas kernels, shards(): pl.pallas_call(functools.partial(kernel, kf_count, kc_count), out_shape=(...  10.5 us
    dot_general x1, matrix products, shards(): lax.dot_general(turned, columns, (((1,), (1,)), ((), ())), preferred_elem...  0.97 us

profile of v3, /device:TPU:0, one launch (start us, length us, event | category | flops | bytes accessed | tf_op | source)
XLA Modules:
  0.0 11.5 jit_solution(10572077006410553169)
XLA Ops:
  0.0 10.5 %shard_map.37 = (bf16[256,256]{1,0:T(8,128)(2,1)S(1)}, bf16[512,256]{1,0:T(8,128)(2,1)S(1)}) custom-call(bf16[32,256]{1,0:T(8,128)(2,1)} %kernel_hbm.1, bf16[4,256]{1,0:T(4,128)(2,1)} %coef_hbm.1, s32[128]{0:T(128)} %near_hbm.1), custom_call_target="tpu_custom_call" | custom-call | tf_op jit(solution)/shard_map/pallas_call | solution.py:239
  10.5 1.0 %convolution_convert_fusion = bf16[256,512]{1,0:T(8,128)(2,1)} fusion(bf16[256,256]{1,0:T(8,128)(2,1)S(1)} %get-tuple-element.7, bf16[512,256]{1,0:T(8,128)(2,1)S(1)} %get-tuple-element.8), kind=kOutput, calls=%fused_computation | convolution fusion | flops 67239936 | bytes 655360 | tf_op jit(solution)/shard_map/dot_general | solution.py:268
